TPU v7x, 256 devices: a whole 4x4x8 slice. The times are simulated.
256 devices in a mesh: dp: 8 (over z_lo, x), fsdp: 32 (over y, z_hi, core).
Axes of the slice: x: 4, y: 4, z: 8 (z_hi: 4, z_lo: 2; z = z_hi * 2 + z_lo), core: 2. Of those that a mesh axis runs over, the one named last changes fastest.
Arguments:
- glu_out: bfloat16 [256, 768, 1536], P(('dp', 'fsdp')), may hold values from -6 to 6
- residual_in: bfloat16 [256, 768, 1536], P(('dp', 'fsdp')), may hold values from -6 to 6
- cotangent: bfloat16 [256, 768, 1536], P(('dp', 'fsdp')), may hold values from -6 to 6
- lengths: int32 [256], P(('dp', 'fsdp')), may hold values from 192 to 768, as said below
- conv_kernel: bfloat16 [5, 1536], P(None, 'fsdp'), may hold values from -2.5 to 2.5
- norm_gain: bfloat16 [1536], P('fsdp'), may hold values from 0.099609375 to 1.8984375
- norm_bias: bfloat16 [1536], P('fsdp'), may hold values from -3 to 3
- proj_weight: bfloat16 [1536, 1536], P('fsdp'), may hold values from -0.15625 to 0.15625
Outputs:
- block_out: bfloat16 [256, 768, 1536], P(('dp', 'fsdp'))
- glu_grad: bfloat16 [256, 768, 1536], P(('dp', 'fsdp'))
- proj_grad: float32 [1536, 1536], P('fsdp')
- kernel_grad: float32 [5, 1536], P(None, 'fsdp')
- norm_grads: float32 [2, 1536], P(None, 'fsdp')
Inputs may be any that keep to these rules, and one draw needn't show every extreme that they name: `lengths`: lengths are drawn independently for each utterance; one utterance has all 768 frames valid and another has 192.
All inputs are finite; a program needn't handle non-finite values.
Results may differ from a plain program's by a relative error of at most 0.0029.
Values may be sent and summed in bfloat16 or wider, within the bound.
No kernel may reach another device: no remote copies, remote signals or barrier semaphores. Data moves between devices by JAX's collectives and lax.ppermute only.
A program may use at most 128 MiB of HBM per device.

v0:
```python
import jax
import jax.numpy as jnp
from jax import lax
from jax.sharding import PartitionSpec as P

TAPS = 5


def local(glu_out, residual_in, cotangent, lengths, conv_kernel, norm_gain, norm_bias, proj_weight):
    kernel, gain, bias = (
        lax.all_gather(conv_kernel, "fsdp", axis=1, tiled=True),
        lax.all_gather(norm_gain, "fsdp", axis=0, tiled=True),
        lax.all_gather(norm_bias, "fsdp", axis=0, tiled=True),
    )
    kernel = kernel.astype(jnp.float32)
    gain = gain.astype(jnp.float32)
    bias = bias.astype(jnp.float32)
    utt_count, frame_count, width = glu_out.shape
    rows_count = utt_count * frame_count
    half = (TAPS - 1) // 2
    frame_ids = jnp.arange(frame_count, dtype=jnp.int32)
    mask = (frame_ids[None, :] < lengths[:, None]).astype(jnp.float32)[:, :, None]
    masked = glu_out.astype(jnp.float32) * mask
    padded = jnp.pad(masked, ((0, 0), (half, half), (0, 0)))
    conv = jnp.zeros_like(masked)
    for k in range(TAPS):
        conv = conv + kernel[k] * padded[:, k : k + frame_count, :]
    mean_val = jnp.mean(conv, axis=-1, keepdims=True)
    centred = conv - mean_val
    rstd = lax.rsqrt(jnp.mean(centred * centred, axis=-1, keepdims=True) + 1e-05)
    normed = centred * rstd
    pre = normed * gain + bias
    sig = jax.nn.sigmoid(pre)
    swished = (pre * sig).astype(jnp.bfloat16)
    flat = swished.reshape(rows_count, width)
    cols = flat
    proj = jnp.dot(
        cols,
        lax.all_gather(proj_weight, "fsdp", axis=0, tiled=True),
        preferred_element_type=jnp.float32,
    )
    proj = proj.reshape(glu_out.shape)
    block_out = (residual_in.astype(jnp.float32) + mask * proj).astype(jnp.bfloat16)
    gout = (cotangent.astype(jnp.float32) * mask).astype(jnp.bfloat16)
    gflat = gout.reshape(rows_count, width)
    gswish = lax.dot_general(
        gflat,
        lax.all_gather(proj_weight, "fsdp", axis=0, tiled=True),
        (((1,), (1,)), ((), ())),
        preferred_element_type=jnp.float32,
    )
    gswish = gswish.reshape(glu_out.shape)
    gpre = gswish * sig * (1.0 + pre * (1.0 - sig))
    gain_term = jnp.sum(gpre * normed, axis=(0, 1))
    bias_term = jnp.sum(gpre, axis=(0, 1))
    gnorm = gpre * gain
    gconv = rstd * (
        gnorm
        - jnp.mean(gnorm, axis=-1, keepdims=True)
        - normed * jnp.mean(gnorm * normed, axis=-1, keepdims=True)
    )
    kernel_terms = jnp.stack(
        [jnp.sum(gconv * padded[:, k : k + frame_count, :], axis=(0, 1)) for k in range(TAPS)]
    )
    gpad = jnp.pad(gconv, ((0, 0), (half, half), (0, 0)))
    gin = jnp.zeros_like(gconv)
    for k in range(TAPS):
        gin = gin + kernel[k] * gpad[:, TAPS - 1 - k : TAPS - 1 - k + frame_count, :]
    glu_grad = (gin * mask).astype(jnp.bfloat16)
    small = jnp.concatenate([kernel_terms, gain_term[None], bias_term[None]], axis=0)
    small_share = lax.psum_scatter(small, "fsdp", scatter_dimension=1, tiled=True)
    cols = flat
    share = lax.psum_scatter(
        lax.dot_general(cols, gflat, (((0,), (0,)), ((), ())), preferred_element_type=jnp.float32),
        "fsdp",
        scatter_dimension=0,
        tiled=True,
    )
    proj_grad, small_total = lax.psum((share, small_share), "dp")
    return (block_out, glu_grad, proj_grad, small_total[:TAPS], small_total[TAPS:])


def solution(mesh):
    placed = (
        P(("dp", "fsdp"), None, None),
        P(("dp", "fsdp"), None, None),
        P(("dp", "fsdp"), None, None),
        P(("dp", "fsdp")),
        P(None, "fsdp"),
        P("fsdp"),
        P("fsdp"),
        P("fsdp", None),
    )
    return jax.shard_map(
        local,
        mesh=mesh,
        in_specs=placed,
        out_specs=(
            P(("dp", "fsdp"), None, None),
            P(("dp", "fsdp"), None, None),
            P("fsdp", None),
            P(None, "fsdp"),
            P(None, "fsdp"),
        ),
        check_vma=False,
    )
```

profile of v0, /device:TPU:8, one launch (start us, length us, event | category | flops | bytes accessed | tf_op | source)
XLA Modules:
  0.0 451.1 jit_solution(17166549743025896024)
XLA Ops:
  7.2 0.0 all-gather.3.cloned.1.call-start
  7.2 0.7 all-gather.3.cloned.1.call-update
  7.9 0.0 reduce-scatter.5.cloned.1.call-start
  8.6 1.3 dynamic-slice
  10.5 0.9 dynamic-update-slice.1
  11.4 0.8 dynamic-update-slice
  12.2 68.2 %all-reduce.4 = (bf16[1536]{0:T(1024)(128)(2,1)S(1)}, bf16[1536]{0:T(1024)(128)(2,1)S(1)}) all-reduce(bf16[1536]{0:T(1024)(128)(2,1)S(1)} %dynamic-update-slice.1, bf16[1536]{0:T(1024)(128)(2,1)S(1)} %dynamic-update-slice), channel_id=1, replica_groups=mesh['dp'=8,'fsdp'=32] {'fsdp'}, use_global_device_ids=true, to_apply=%add.3 | all-reduce | flops 3072 | bytes 12288
  80.5 47.1 %all-gather = bf16[32,48,5]{1,2,0:T(8,128)(2,1)S(1)} all-gather(bf16[1,48,5]{1,2,0:T(8,128)(2,1)} %bitcast.37), channel_id=1, replica_groups=mesh['dp'=8,'fsdp'=32] {'fsdp'}, dimensions={0}, use_global_device_ids=true | all-gather | bytes 15840 | tf_op jit(solution)/shard_map/all_gather | solution.py:11
  127.6 0.1 reshape.110
  127.7 0.1 slice_reduce_fusion.4
  127.8 2.0 convert_multiply_fusion
  129.9 0.0 copy-start.1
  129.9 3.6 fusion.10
  133.5 0.0 copy-done.1
  133.5 0.0 copy-start
  133.5 0.0 copy-start.4
  133.5 0.6 multiply_reduce_fusion.7
  134.2 1.8 copy-done
  135.9 1.0 copy-done.4
  136.9 7.2 %fusion.4 = f32[1536,1536]{1,0:T(8,128)} fusion(bf16[1,768,1536]{2,1,0:T(8,128)(2,1)S(1)} %copy-done.4, f32[768]{0:T(1024)S(1)} %fusion.9, f32[1,768,1536]{2,1,0:T(8,128)S(1)} %get-tuple-element.23, f32[1536]{0:T(1024)S(1)} %convert_element_type.47, f32[1536]{0:T(1024)S(1)} %convert_element_type.46, f32[768]{0:T(1024)S(1)} %add_rsqrt_fusion, ...), kind=kOutput, calls=%fused_computation.28 | convolution fusion | flops 3638034432 | bytes 16536576 | tf_op jit(solution)/shard_map/dot_general | solution.py:74
  144.1 0.0 reduce-scatter.5.cloned.1.call-update
  144.2 0.0 copy-start.2
  144.2 0.2 reduce-scatter.7.cloned.1.call-start
  144.4 0.0 all-gather.3.cloned.1.call-done
  144.4 10.1 %multiply_reduce_fusion = (f32[1536]{0:T(1024)S(1)}, f32[768]{0:T(1024)S(1)}, f32[768]{0:T(1024)S(1)}, f32[1536]{0:T(1024)S(1)}, f32[1,768,1536]{2,1,0:T(8,128)S(1)}) fusion(f32[1,768,1536]{2,1,0:T(8,128)} %copy-done, f32[768]{0:T(1024)S(1)} %add_rsqrt_fusion, f32[768]{0:T(1024)S(1)} %broadcast_multiply_fusion.2, f32[1536]{0:T(1024)S(1)} %convert_element_type.46, ...), kind=kOutput, calls=%fused_computation.4 | convolution fusion | flops 3649826304 | bytes 16555008 | tf_op jit(solution)/shard_map/dot_general | solution.py:46
  154.6 0.0 copy-done.2
  154.6 17.7 %multiply_reduce_fusion.1 = (f32[1536]{0:T(1024)S(1)}, f32[1536]{0:T(1024)S(1)}, f32[1536]{0:T(1024)S(1)}, f32[1536]{0:T(1024)S(1)}, f32[1536]{0:T(1024)S(1)}, /*index=5*/f32[1,768,1536]{2,1,0:T(8,128)}) fusion(f32[1,768,1536]{2,1,0:T(8,128)} %copy-done.1, f32[768]{0:T(1024)S(1)} %fusion.9, bf16[1,768,1536]{2,1,0:T(8,128)(2,1)S(1)} %copy-done.2, ...), kind=kLoop, calls=%fused_computation.5 | loop fusion | flops 22405632 | bytes 21285888 | tf_op jit(solution)/shard_map/reduce_sum | solution.py:63
  172.4 0.1 concatenate.3
  172.4 1.2 copy.16
  173.6 0.0 reduce-scatter.7.cloned.1.call-update
  173.7 0.0 all-reduce.7.cloned.1.call-start
  173.7 10.8 %fusion.1 = bf16[1,768,1536]{2,1,0:T(8,128)(2,1)} fusion(bf16[1,768,1536]{2,1,0:T(8,128)(2,1)} %param.9, bf16[1536,1536]{1,0:T(8,128)(2,1)} %all-gather.3.cloned.1.call-done, f32[768]{0:T(1024)S(1)} %fusion.9, f32[1,768,1536]{2,1,0:T(8,128)} %copy-done, f32[1536]{0:T(1024)S(1)} %convert_element_type.47, f32[1536]{0:T(1024)S(1)} %convert_element_type.46, ...), kind=kOutput, calls=%fused_computation.3 | convolution fusion | flops 3639214080 | bytes 14177280 | tf_op jit(solution)/shard_map/dot_general | solution.py:37
  184.5 86.9 %reduce-scatter.5.cloned.1.call-done = f32[48,1536]{1,0:T(8,128)} async-done(((f32[1536,1536]{1,0:T(8,128)}), f32[48,1536]{1,0:T(8,128)}) %reduce-scatter.5.cloned.1.call-update) | async-done | bytes 294928 | tf_op jit(solution)/shard_map/reduce_scatter | solution.py:73
  271.4 0.0 all-reduce.7.cloned.1.call-update
  271.4 12.9 %multiply_convert_fusion = bf16[1,768,1536]{2,1,0:T(8,128)(2,1)} fusion(f32[1,768,1536]{2,1,0:T(8,128)} %get-tuple-element.21, f32[1536]{0:T(1024)S(1)} %get-tuple-element.15, f32[1536]{0:T(1024)S(1)} %get-tuple-element.16, f32[1536]{0:T(1024)S(1)} %get-tuple-element.17, f32[1536]{0:T(1024)S(1)} %get-tuple-element.18, f32[768]{0:T(1024)S(1)} %fusion.9, ...), kind=kLoop, calls=%fused_computation.10 | loop fusion | flops 12976128 | bytes 7111680 | tf_op jit(solution)/shard_map/convert_element_type | solution.py:69
  284.3 78.1 %reduce-scatter.7.cloned.1.call-done = f32[48,7]{1,0:T(8,128)} async-done(((f32[1536,7]{1,0:T(8,128)}), f32[48,7]{1,0:T(8,128)}) %reduce-scatter.7.cloned.1.call-update) | async-done | bytes 1360
  362.3 0.8 copy.17
  363.1 18.7 %psum.15 = f32[7,48]{1,0:T(8,128)S(1)} all-reduce(f32[7,48]{1,0:T(8,128)S(1)} %copy.17), channel_id=1, replica_groups=mesh['dp'=8,'fsdp'=32] {'dp'}, use_global_device_ids=true, to_apply=%region_14.15 | all-reduce | flops 336 | bytes 2688 | tf_op jit(solution)/shard_map/psum | solution.py:79
  381.8 0.0 copy-start.3
  381.9 0.6 slice.71
  382.4 60.4 %all-reduce.7.cloned.1.call-done = f32[48,1536]{1,0:T(8,128)} async-done(((f32[48,1536]{1,0:T(8,128)}), f32[48,1536]{1,0:T(8,128)}) %all-reduce.7.cloned.1.call-update) | async-done | bytes 294928 | tf_op jit(solution)/shard_map/psum | solution.py:79
  442.8 1.7 copy.23
  444.5 0.0 copy-done.3
  (16 shorter events, 0.1 us)
Async XLA Ops:
  7.2 137.3 %all-gather.3.cloned.1.call-start = ((), (), s32[]{:S(2)}) async-start(), calls=%async_computation.2 | async-start | bytes 4866048 | tf_op jit(solution)/shard_map/all_gather | solution.py:39
  7.9 263.5 %reduce-scatter.5.cloned.1.call-start = ((), (), s32[]{:S(2)}) async-start(), calls=%async_computation.3 | async-start | bytes 9732096 | tf_op jit(solution)/shard_map/reduce_scatter | solution.py:73
  129.9 3.6 copy-start.1
  133.5 2.4 copy-start
  133.5 3.4 copy-start.4
  144.2 10.4 %copy-start.2 = (bf16[1,768,1536]{2,1,0:T(8,128)(2,1)S(1)}, bf16[1,768,1536]{2,1,0:T(8,128)(2,1)}, u32[]{:S(2)}) copy-start(bf16[1,768,1536]{2,1,0:T(8,128)(2,1)} %param.8) | copy-start | bytes 7077892
  144.2 218.2 %reduce-scatter.7.cloned.1.call-start = ((), (), s32[]{:S(2)}) async-start(), calls=%async_computation.5 | async-start | bytes 811008
  173.7 269.2 %all-reduce.7.cloned.1.call-start = ((), (), s32[]{:S(2)}) async-start(), calls=%async_computation.4 | async-start | bytes 589824 | tf_op jit(solution)/shard_map/psum | solution.py:79
  381.8 62.7 %copy-start.3 = (f32[7,48]{1,0:T(8,128)}, f32[7,48]{1,0:T(8,128)S(1)}, u32[]{:S(2)}) copy-start(f32[7,48]{1,0:T(8,128)S(1)} %psum.15) | copy-start | bytes 4036
Sparse Core Ops, SparseCore 0:
  10.5 66.0 all-gather.2
  144.3 127.0 reduce-scatter.4
  275.6 86.6 reduce-scatter.6
  365.0 77.7 all-reduce.6
where the time goes:
time: 451 us
  waiting for transfers between devices  226 us (50%)
  blocking collectives  134 us (30%)
  other arithmetic  36.9 us (8%)
  matrix products  28.1 us (6%)
  between operations  15.3 us (3%)
  local copies, waits for them, and re-layouts  10.3 us (2%)
    reduce_scatter x1, waiting for transfers between devices, local(): lax.psum_scatter(lax.dot_general(cols, gflat, (((0,), (0,)), ((), ())), p...  86.9 us
    unnamed x5, waiting for transfers between devices  78.8 us
    unnamed x1, blocking collectives  68.2 us
    psum x1, waiting for transfers between devices, local(): proj_grad, small_total = lax.psum((share, small_share), 'dp')  60.4 us
    all_gather x1, blocking collectives, local(): lax.all_gather(conv_kernel, 'fsdp', axis=1, tiled=True)  47.1 us
    psum x1, blocking collectives, local(): proj_grad, small_total = lax.psum((share, small_share), 'dp')  18.7 us
    reduce_sum x1, other arithmetic, local(): jnp.sum(gconv * padded[:, k:k + frame_count, :], axis=(0, 1))  17.7 us
    convert_element_type x1, other arithmetic, local(): glu_grad = (gin * mask).astype(jnp.bfloat16)  12.9 us
  transfers between devices with their start and end apart: 4, of which 3 were waited for; matrix products, arithmetic and copies ran while one was open for 16% of the time, Pallas kernels for 0%

commit v1 on v0

--- a/solution.py
+++ b/solution.py
@@ -8,7 +8,9 @@
 
 def local(glu_out, residual_in, cotangent, lengths, conv_kernel, norm_gain, norm_bias, proj_weight):
     kernel, gain, bias = (
-        lax.all_gather(conv_kernel, "fsdp", axis=1, tiled=True),
+        jnp.concatenate(
+            lax.all_to_all(jnp.stack([conv_kernel] * lax.axis_size("fsdp")), "fsdp", 0, 0), axis=1
+        ),
         lax.all_gather(norm_gain, "fsdp", axis=0, tiled=True),
         lax.all_gather(norm_bias, "fsdp", axis=0, tiled=True),
     )

time: 451 us -> 429 us (0.951)
  blocking collectives: 134 us -> 86.8 us
  starting transfers between devices: 0.34 us -> 12 us
  other arithmetic: 36.9 us -> 46.2 us
    all_gather x1 -> x0, blocking collectives: 47.1 us -> none  [local(): lax.all_gather(conv_kernel, 'fsdp', axis=1, tiled=True)]
    all_to_all x0 -> x1, starting transfers between devices: none -> 11.7 us  [local(): lax.all_to_all(jnp.stack([conv_kernel] * lax.axis_size('fsdp')), 'fsdp',...]
    reduce_sum x1, other arithmetic: 3.62 us -> 10.6 us  [local(): mean_val = jnp.mean(conv, axis=-1, keepdims=True)]
    unnamed x18 -> x22, local copies, waits for them, and re-layouts: 9.43 us -> 7.56 us
  transfers between devices with their start and end apart: 4 -> 5, of which waited for: 3 -> 3; matrix products, arithmetic and copies ran while one was open for 16% -> 19% of each run, Pallas kernels for 0% -> 0%
where the time goes in v1:
time: 429 us
  waiting for transfers between devices  230 us (54%)
  blocking collectives  86.8 us (20%)
  other arithmetic  46.2 us (11%)
  matrix products  28.1 us (7%)
  between operations  15.3 us (4%)
  starting transfers between devices  12 us (3%)
  local copies, waits for them, and re-layouts  10.2 us (2%)
    reduce_scatter x1, waiting for transfers between devices, local(): lax.psum_scatter(lax.dot_general(cols, gflat, (((0,), (0,)), ((), ())), p...  90.7 us
    unnamed x5, waiting for transfers between devices  78.9 us
    unnamed x1, blocking collectives  68.1 us
    psum x1, waiting for transfers between devices, local(): proj_grad, small_total = lax.psum((share, small_share), 'dp')  60.4 us
    psum x1, blocking collectives, local(): proj_grad, small_total = lax.psum((share, small_share), 'dp')  18.7 us
    reduce_sum x1, other arithmetic, local(): jnp.sum(gconv * padded[:, k:k + frame_count, :], axis=(0, 1))  17.8 us
    convert_element_type x1, other arithmetic, local(): glu_grad = (gin * mask).astype(jnp.bfloat16)  12.9 us
    all_to_all x1, starting transfers between devices, local(): lax.all_to_all(jnp.stack([conv_kernel] * lax.axis_size('fsdp')), 'fsdp',...  11.7 us
  transfers between devices with their start and end apart: 5, of which 3 were waited for; matrix products, arithmetic and copies ran while one was open for 19% of the time, Pallas kernels for 0%

profile of v1, /device:TPU:8, one launch (start us, length us, event | category | flops | bytes accessed | tf_op | source)
XLA Modules:
  0.0 428.7 jit_solution(6881206299707910251)
XLA Ops:
  7.2 0.0 copy-start.6
  7.2 0.0 copy-start.4
  7.2 0.0 copy-start.5
  7.2 0.0 all-gather.2.cloned.1.call-start
  7.2 0.7 all-gather.2.cloned.1.call-update
  7.9 1.3 stack.12
  9.3 11.7 %all-to-all-start = ((bf16[32,5,48]{2,1,0:T(8,128)(2,1)}), bf16[32,5,48]{2,1,0:T(8,128)(2,1)S(1)}, u32[]{:S(2)}, u32[]{:S(2)}) async-start(bf16[32,5,48]{2,1,0:T(8,128)(2,1)} %stack.12), calls=%async_computation | async-start | bytes 131072 | tf_op jit(solution)/shard_map/all_to_all | solution.py:12
  21.0 0.0 reduce-scatter.5.cloned.1.call-start
  21.7 4.3 convert_multiply_fusion
  26.0 0.0 copy-done.6
  26.0 0.6 dynamic-slice
  27.2 0.2 dynamic-update-slice.1
  27.5 0.2 dynamic-update-slice
  27.7 68.1 %all-reduce.4 = (bf16[1536]{0:T(1024)(128)(2,1)S(1)}, bf16[1536]{0:T(1024)(128)(2,1)S(1)}) all-reduce(bf16[1536]{0:T(1024)(128)(2,1)S(1)} %dynamic-update-slice.1, bf16[1536]{0:T(1024)(128)(2,1)S(1)} %dynamic-update-slice), channel_id=1, replica_groups=mesh['dp'=8,'fsdp'=32] {'fsdp'}, use_global_device_ids=true, to_apply=%add.3 | all-reduce | flops 3072 | bytes 12288
  95.9 0.0 all-to-all-done
  95.9 0.2 slice_reduce_fusion.4
  96.1 0.1 mul.184
  96.2 0.1 mul.198
  96.3 0.1 mul.195
  96.4 0.1 mul.192
  96.4 0.1 mul.189
  96.5 10.6 %fusion.10 = (f32[768]{0:T(1024)S(1)}, f32[1,768,1536]{2,1,0:T(8,128)S(1)}) fusion(f32[1536]{0:T(1024)S(1)} %mul.198, f32[1536]{0:T(1024)S(1)} %mul.195, f32[1,768,1536]{2,1,0:T(8,128)} %convert_multiply_fusion, f32[1536]{0:T(1024)S(1)} %mul.192, f32[1536]{0:T(1024)S(1)} %mul.189, f32[1536]{0:T(1024)S(1)} %mul.184), kind=kLoop, calls=%fused_computation.43 | loop fusion | flops 11795712 | bytes 9470976 | tf_op jit(solution)/shard_map/reduce_sum | solution.py:30
  107.1 0.0 copy-start
  107.1 0.0 copy-start.3
  107.1 0.6 multiply_reduce_fusion.7
  107.7 1.8 copy-done
  109.5 1.0 copy-done.3
  110.5 7.2 %fusion.4 = f32[1536,1536]{1,0:T(8,128)} fusion(bf16[1,768,1536]{2,1,0:T(8,128)(2,1)S(1)} %copy-done.3, f32[768]{0:T(1024)S(1)} %fusion.9, f32[1,768,1536]{2,1,0:T(8,128)S(1)} %get-tuple-element.23, f32[1536]{0:T(1024)S(1)} %convert_element_type.52, f32[1536]{0:T(1024)S(1)} %convert_element_type.51, f32[768]{0:T(1024)S(1)} %add_rsqrt_fusion, ...), kind=kOutput, calls=%fused_computation.28 | convolution fusion | flops 3638034432 | bytes 16536576 | tf_op jit(solution)/shard_map/dot_general | solution.py:76
  117.7 0.0 reduce-scatter.5.cloned.1.call-update
  117.7 0.0 copy-start.1
  117.7 0.2 reduce-scatter.7.cloned.1.call-start
  117.9 0.0 all-gather.2.cloned.1.call-done
  118.0 10.1 %multiply_reduce_fusion = (f32[1536]{0:T(1024)S(1)}, f32[768]{0:T(1024)S(1)}, f32[768]{0:T(1024)S(1)}, f32[1536]{0:T(1024)S(1)}, f32[1,768,1536]{2,1,0:T(8,128)S(1)}) fusion(f32[1,768,1536]{2,1,0:T(8,128)} %copy-done, f32[768]{0:T(1024)S(1)} %add_rsqrt_fusion, f32[768]{0:T(1024)S(1)} %broadcast_multiply_fusion.2, f32[1536]{0:T(1024)S(1)} %convert_element_type.51, ...), kind=kOutput, calls=%fused_computation.4 | convolution fusion | flops 3649826304 | bytes 16555008 | tf_op jit(solution)/shard_map/dot_general | solution.py:48
  128.2 17.8 %multiply_reduce_fusion.1 = (f32[1536]{0:T(1024)S(1)}, f32[1536]{0:T(1024)S(1)}, f32[1536]{0:T(1024)S(1)}, f32[1536]{0:T(1024)S(1)}, f32[1536]{0:T(1024)S(1)}, /*index=5*/f32[1,768,1536]{2,1,0:T(8,128)}) fusion(f32[1,768,1536]{2,1,0:T(8,128)} %convert_multiply_fusion, f32[768]{0:T(1024)S(1)} %fusion.9, bf16[1,768,1536]{2,1,0:T(8,128)(2,1)S(1)} %copy-done.1, ...), kind=kLoop, calls=%fused_computation.5 | loop fusion | flops 22405632 | bytes 21285888 | tf_op jit(solution)/shard_map/reduce_sum | solution.py:65
  146.1 0.1 concatenate.3
  146.1 1.2 copy.13
  147.3 0.0 reduce-scatter.7.cloned.1.call-update
  147.4 0.0 all-reduce.7.cloned.1.call-start
  147.4 10.8 %fusion.1 = bf16[1,768,1536]{2,1,0:T(8,128)(2,1)} fusion(bf16[1,768,1536]{2,1,0:T(8,128)(2,1)} %param.9, bf16[1536,1536]{1,0:T(8,128)(2,1)} %all-gather.2.cloned.1.call-done, f32[768]{0:T(1024)S(1)} %fusion.9, f32[1,768,1536]{2,1,0:T(8,128)} %copy-done, f32[1536]{0:T(1024)S(1)} %convert_element_type.52, f32[1536]{0:T(1024)S(1)} %convert_element_type.51, ...), kind=kOutput, calls=%fused_computation.3 | convolution fusion | flops 3639214080 | bytes 14177280 | tf_op jit(solution)/shard_map/dot_general | solution.py:39
  158.2 90.7 %reduce-scatter.5.cloned.1.call-done = f32[48,1536]{1,0:T(8,128)} async-done(((f32[1536,1536]{1,0:T(8,128)}), f32[48,1536]{1,0:T(8,128)}) %reduce-scatter.5.cloned.1.call-update) | async-done | bytes 294928 | tf_op jit(solution)/shard_map/reduce_scatter | solution.py:75
  248.9 0.0 all-reduce.7.cloned.1.call-update
  248.9 12.9 %multiply_convert_fusion = bf16[1,768,1536]{2,1,0:T(8,128)(2,1)} fusion(f32[1,768,1536]{2,1,0:T(8,128)} %get-tuple-element.21, f32[1536]{0:T(1024)S(1)} %mul.198, f32[1536]{0:T(1024)S(1)} %mul.195, f32[1536]{0:T(1024)S(1)} %mul.192, f32[1536]{0:T(1024)S(1)} %mul.189, f32[768]{0:T(1024)S(1)} %fusion.9, f32[1536]{0:T(1024)S(1)} %mul.184), kind=kLoop, calls=%fused_computation.10 | loop fusion | flops 12976128 | bytes 7111680 | tf_op jit(solution)/shard_map/convert_element_type | solution.py:71
  261.8 78.2 %reduce-scatter.7.cloned.1.call-done = f32[48,7]{1,0:T(8,128)} async-done(((f32[1536,7]{1,0:T(8,128)}), f32[48,7]{1,0:T(8,128)}) %reduce-scatter.7.cloned.1.call-update) | async-done | bytes 1360
  340.0 0.8 copy.14
  340.8 18.7 %psum.15 = f32[7,48]{1,0:T(8,128)S(1)} all-reduce(f32[7,48]{1,0:T(8,128)S(1)} %copy.14), channel_id=1, replica_groups=mesh['dp'=8,'fsdp'=32] {'dp'}, use_global_device_ids=true, to_apply=%region_14.15 | all-reduce | flops 336 | bytes 2688 | tf_op jit(solution)/shard_map/psum | solution.py:81
  359.5 0.6 slice.76
  360.1 60.4 %all-reduce.7.cloned.1.call-done = f32[48,1536]{1,0:T(8,128)} async-done(((f32[48,1536]{1,0:T(8,128)}), f32[48,1536]{1,0:T(8,128)}) %all-reduce.7.cloned.1.call-update) | async-done | bytes 294928 | tf_op jit(solution)/shard_map/psum | solution.py:81
  420.5 1.7 copy.19
  (21 shorter events, 0.1 us)
Async XLA Ops:
  7.2 18.8 %copy-start.6 = (u32[256]{0:T(256)S(1)}, u32[256]{0:T(256)}, u32[]{:S(2)}) copy-start(u32[256]{0:T(256)} %constant.28) | copy-start | bytes 3076
  7.2 20.0 %copy-start.4 = (bf16[48]{0:T(256)(128)(2,1)S(1)}, bf16[48]{0:T(256)(128)(2,1)}, u32[]{:S(2)}) copy-start(bf16[48]{0:T(256)(128)(2,1)} %param.14) | copy-start | bytes 292
  7.2 20.3 %copy-start.5 = (bf16[48]{0:T(256)(128)(2,1)S(1)}, bf16[48]{0:T(256)(128)(2,1)}, u32[]{:S(2)}) copy-start(bf16[48]{0:T(256)(128)(2,1)} %param.13) | copy-start | bytes 292
  7.2 110.8 %all-gather.2.cloned.1.call-start = ((), (), s32[]{:S(2)}) async-start(), calls=%async_computation.3 | async-start | bytes 4866048 | tf_op jit(solution)/shard_map/all_gather | solution.py:41
  9.3 86.6 %all-to-all-start = ((bf16[32,5,48]{2,1,0:T(8,128)(2,1)}), bf16[32,5,48]{2,1,0:T(8,128)(2,1)S(1)}, u32[]{:S(2)}, u32[]{:S(2)}) async-start(bf16[32,5,48]{2,1,0:T(8,128)(2,1)} %stack.12), calls=%async_computation | async-start | bytes 131072 | tf_op jit(solution)/shard_map/all_to_all | solution.py:12
  21.0 227.9 %reduce-scatter.5.cloned.1.call-start = ((), (), s32[]{:S(2)}) async-start(), calls=%async_computation.4 | async-start | bytes 9732096 | tf_op jit(solution)/shard_map/reduce_scatter | solution.py:75
  107.1 2.4 copy-start
  107.1 3.4 copy-start.3
  117.7 10.4 %copy-start.1 = (bf16[1,768,1536]{2,1,0:T(8,128)(2,1)S(1)}, bf16[1,768,1536]{2,1,0:T(8,128)(2,1)}, u32[]{:S(2)}) copy-start(bf16[1,768,1536]{2,1,0:T(8,128)(2,1)} %param.8) | copy-start | bytes 7077892
  117.7 222.3 %reduce-scatter.7.cloned.1.call-start = ((), (), s32[]{:S(2)}) async-start(), calls=%async_computation.6 | async-start | bytes 811008
  147.4 273.1 %all-reduce.7.cloned.1.call-start = ((), (), s32[]{:S(2)}) async-start(), calls=%async_computation.5 | async-start | bytes 589824 | tf_op jit(solution)/shard_map/psum | solution.py:81
  359.5 62.6 %copy-start.2 = (f32[7,48]{1,0:T(8,128)}, f32[7,48]{1,0:T(8,128)S(1)}, u32[]{:S(2)}) copy-start(f32[7,48]{1,0:T(8,128)S(1)} %psum.15) | copy-start | bytes 4036
Sparse Core Ops, SparseCore 0:
  10.6 66.0 all-gather.1
  117.8 131.0 reduce-scatter.4
  253.1 86.8 reduce-scatter.6
  342.7 77.7 all-reduce.6
